TPU v7x, 512 devices: a whole 4x4x16 slice. The times are simulated.
512 devices in a mesh: vocab: 64 (over x, z), batch: 8 (over y, core).
Axes of the slice: x: 4, y: 4, z: 16, core: 2. Of those that a mesh axis runs over, the one named last changes fastest.
Arguments:
- hidden: bfloat16 [1024, 4096], P('batch', 'vocab'), may hold values from -6 to 6
- head_weight: bfloat16 [4096, 65536], P('batch', 'vocab'), may hold values from -0.09375 to 0.09375
- passages: bfloat16 [2048, 65536], P('batch', 'vocab'), may hold values from -6 to 6
- pair_query: int32 [3072], P('batch'), may hold values from 0 to 63
- pair_passage: int32 [3072], P('batch'), may hold values from 0 to 255
- pair_count: int32 [8], P('batch'), may hold values from 128 to 384, as said below
- teacher: float32 [3072], P('batch'), may hold values from -24 to 24
Outputs:
- pooled: bfloat16 [64, 65536], P('batch', 'vocab')
- grad_hidden: bfloat16 [1024, 4096], P('batch', 'vocab')
- loss_value: float32 [], replicated
Inputs may be any that keep to these rules, and one draw needn't show every extreme that they name: `pair_count`: slots of a group at or past its count are padding; some group has all 384 slots live.
All inputs are finite; a program needn't handle non-finite values.
Results may differ from a plain program's by a relative error of at most 0.012.
Values may be sent and summed in bfloat16 or wider, within the bound.
No kernel may reach another device: no remote copies, remote signals or barrier semaphores. Data moves between devices by JAX's collectives and lax.ppermute only.
A program may use at most 64 MiB of HBM per device.

v0:
```python
import math
import jax
import jax.numpy as jnp
from jax import lax
from jax.sharding import PartitionSpec as P

VOCAB = 65536
QLEN = 16


def local(hidden, head_weight, passages, pair_query, pair_passage, pair_count, teacher):
    features = lax.all_gather(hidden, "vocab", axis=1, tiled=True)
    full_head = lax.all_gather(head_weight, "batch", axis=0, tiled=True)
    logits = jnp.dot(features, full_head, preferred_element_type=jnp.float32)
    positive = jnp.maximum(logits, 0.0)
    saturated = jnp.log1p(positive)
    tok_count, col_count = logits.shape
    query_count = tok_count // QLEN
    pooled = saturated.reshape(query_count, QLEN, col_count).sum(1).astype(jnp.bfloat16)
    every_query = lax.all_gather(pooled, "batch", axis=0, tiled=True)
    score_table = jnp.dot(every_query, passages.T, preferred_element_type=jnp.float32)
    partial_value = score_table[pair_query, pair_passage]
    inv_root = 1.0 / math.sqrt(VOCAB)
    slot_count = pair_query.shape[0]
    is_live = jnp.arange(slot_count, dtype=jnp.int32) < pair_count[0]
    scores = lax.psum(partial_value, "vocab") * inv_root
    residual = jnp.where(is_live, scores - teacher, 0.0)
    error_total = lax.psum(jnp.sum(residual * residual), "batch")
    pair_grad = 2.0 * residual * inv_root
    loss_value = error_total / (slot_count * lax.axis_size("batch"))
    query_onehot = (
        pair_query[:, None] == jnp.arange(every_query.shape[0], dtype=jnp.int32)[None, :]
    ).astype(jnp.float32)
    passage_onehot = (
        pair_passage[:, None] == jnp.arange(passages.shape[0], dtype=jnp.int32)[None, :]
    ).astype(jnp.float32)
    pair_table = jnp.dot(
        query_onehot.T, passage_onehot * pair_grad[:, None], precision=lax.Precision.HIGHEST
    )
    table_high = pair_table.astype(jnp.bfloat16)
    table_low = (pair_table - table_high.astype(jnp.float32)).astype(jnp.bfloat16)
    query_terms = jnp.dot(table_high, passages, preferred_element_type=jnp.float32) + jnp.dot(
        table_low, passages, preferred_element_type=jnp.float32
    )
    query_grad = lax.psum_scatter(query_terms, "batch", scatter_dimension=0, tiled=True)
    slope_term = jnp.where(logits > 0, 1.0 / (1.0 + positive), 0.0)
    spread_grad = jnp.broadcast_to(query_grad[:, None, :], (query_count, QLEN, col_count)).reshape(
        tok_count, col_count
    )
    logit_grad = (spread_grad * slope_term).astype(jnp.bfloat16)
    hidden_terms = lax.dot_general(
        logit_grad, full_head, (((1,), (1,)), ((), ())), preferred_element_type=jnp.float32
    )
    grad_hidden = lax.psum_scatter(hidden_terms, "vocab", scatter_dimension=1, tiled=True).astype(
        jnp.bfloat16
    )
    return (pooled, grad_hidden, loss_value)


def solution(mesh):
    in_specs = (
        P("batch", "vocab"),
        P("batch", "vocab"),
        P("batch", "vocab"),
        P("batch"),
        P("batch"),
        P("batch"),
        P("batch"),
    )
    out_specs = (P("batch", "vocab"), P("batch", "vocab"), P())
    return jax.shard_map(local, mesh=mesh, in_specs=in_specs, out_specs=out_specs, check_vma=False)
```

profile of v0, /device:TPU:8, one launch (start us, length us, event | category | flops | bytes accessed | tf_op | source)
XLA Modules:
  0.0 1121.6 jit_solution(13885743366258223101)
XLA Ops:
  7.2 0.0 copy-start
  7.2 0.0 all-gather.3.cloned.1.call-start
  7.2 0.7 all-gather.3.cloned.1.call-update
  7.9 0.0 all-gather.5.cloned.1.call-start
  8.0 0.7 all-gather.5.cloned.1.call-update
  8.7 0.0 reduce-scatter.3.cloned.1.call-start
  9.4 0.7 fusion.12
  10.1 0.0 copy-start.2
  10.1 0.0 copy-start.3
  10.1 0.0 copy-start.4
  10.1 145.1 %all-gather.3.cloned.1.call-done = bf16[128,4096]{0,1:T(8,128)(2,1)} async-done(((bf16[128,64]{0,1:T(8,128)(2,1)}), bf16[128,4096]{0,1:T(8,128)(2,1)}) %all-gather.3.cloned.1.call-update) | async-done | bytes 1048592 | tf_op jit(solution)/shard_map/all_gather | solution.py:12
  155.2 54.9 %all-gather.5.cloned.1.call-done = bf16[4096,1024]{1,0:T(8,128)(2,1)} async-done(((bf16[512,1024]{1,0:T(8,128)(2,1)}), bf16[4096,1024]{1,0:T(8,128)(2,1)}) %all-gather.5.cloned.1.call-update) | async-done | bytes 8388624 | tf_op jit(solution)/shard_map/all_gather | solution.py:13
  210.0 5.2 bitcast_reduce_fusion
  215.2 0.0 copy-start.1
  215.2 11.7 %all_gather.11 = bf16[64,1024]{1,0:T(8,128)(2,1)S(1)} all-gather(bf16[8,1024]{1,0:T(8,128)(2,1)S(1)} %get-tuple-element.5), channel_id=1, replica_groups=mesh['vocab'=64,'batch'=8] {'batch'}, dimensions={0}, use_global_device_ids=true | all-gather | bytes 147456 | tf_op jit(solution)/shard_map/all_gather | solution.py:20
  226.9 0.0 copy-done
  226.9 0.3 fusion.16
  227.2 3.4 gather_fusion
  230.7 144.2 %psum.14 = f32[384]{0:T(512)S(1)} all-reduce(f32[384]{0:T(512)S(1)} %gather_fusion), channel_id=1, replica_groups=mesh['vocab'=64,'batch'=8] {'vocab'}, use_global_device_ids=true, to_apply=%region_1.0 | all-reduce | flops 384 | bytes 3072 | tf_op jit(solution)/shard_map/psum | solution.py:26
  374.9 0.0 copy-done.2
  374.9 0.6 multiply_reduce_fusion
  375.5 0.0 copy-done.3
  375.5 0.0 copy-done.4
  375.5 0.5 fusion.1
  376.0 0.2 fusion.8
  376.2 0.9 convolution_add_fusion
  377.2 0.0 reduce-scatter.3.cloned.1.call-update
  377.2 0.0 reduce-scatter.5.cloned.1.call-start
  377.2 24.6 %reduce-scatter.3.cloned.1.call-done = f32[8,1024]{1,0:T(8,128)} async-done(((f32[64,1024]{1,0:T(8,128)}), f32[8,1024]{1,0:T(8,128)}) %reduce-scatter.3.cloned.1.call-update) | async-done | bytes 32784 | tf_op jit(solution)/shard_map/reduce_scatter | solution.py:45
  401.9 0.9 fusion
  402.7 7.1 fusion.17
  409.8 0.0 copy-done.1
  409.8 0.0 reduce-scatter.5.cloned.1.call-update
  409.9 14.5 %psum.15 = f32[]{:T(128)} all-reduce(f32[]{:T(128)} %get-tuple-element.3), channel_id=1, replica_groups=mesh['vocab'=64,'batch'=8] {'batch'}, use_global_device_ids=true, to_apply=%region_5.6 | all-reduce | flops 1 | bytes 8 | tf_op jit(solution)/shard_map/psum | solution.py:28
  425.0 687.6 %reduce-scatter.5.cloned.1.call-done = f32[128,64]{0,1:T(8,128)} async-done(((f32[128,4096]{0,1:T(8,128)}), f32[128,64]{0,1:T(8,128)}) %reduce-scatter.5.cloned.1.call-update) | async-done | bytes 32784 | tf_op jit(solution)/shard_map/reduce_scatter | solution.py:54
  1112.6 1.4 convert_element_type.25
Async XLA Ops:
  7.2 219.8 %copy-start = (bf16[256,1024]{1,0:T(8,128)(2,1)S(1)}, bf16[256,1024]{1,0:T(8,128)(2,1)}, u32[]{:S(2)}) copy-start(bf16[256,1024]{1,0:T(8,128)(2,1)} %param.9) | copy-start | bytes 1572868
  7.2 148.0 %all-gather.3.cloned.1.call-start = ((), (), s32[]{:S(2)}) async-start(), calls=%async_computation.2 | async-start | bytes 1064960 | tf_op jit(solution)/shard_map/all_gather | solution.py:12
  7.9 202.1 %all-gather.5.cloned.1.call-start = ((), (), s32[]{:S(2)}) async-start(), calls=%async_computation.3 | async-start | bytes 9437184 | tf_op jit(solution)/shard_map/all_gather | solution.py:13
  8.7 393.2 %reduce-scatter.3.cloned.1.call-start = ((), (), s32[]{:S(2)}) async-start(), calls=%async_computation.4 | async-start | bytes 294912 | tf_op jit(solution)/shard_map/reduce_scatter | solution.py:45
  10.1 364.8 %copy-start.2 = (f32[384]{0:T(512)S(1)}, f32[384]{0:T(512)}, u32[]{:S(2)}) copy-start(f32[384]{0:T(512)} %param.13) | copy-start | bytes 4612
  10.1 365.4 %copy-start.3 = (s32[384]{0:T(512)S(1)}, s32[384]{0:T(512)}, u32[]{:S(2)}) copy-start(s32[384]{0:T(512)} %param.10) | copy-start | bytes 4612
  10.1 365.4 %copy-start.4 = (s32[384]{0:T(512)S(1)}, s32[384]{0:T(512)}, u32[]{:S(2)}) copy-start(s32[384]{0:T(512)} %param.11) | copy-start | bytes 4612
  215.2 194.6 %copy-start.1 = (bf16[8,1024]{1,0:T(8,128)(2,1)}, bf16[8,1024]{1,0:T(8,128)(2,1)S(1)}, u32[]{:S(2)}) copy-start(bf16[8,1024]{1,0:T(8,128)(2,1)S(1)} %get-tuple-element.5) | copy-start | bytes 49156
  377.2 735.4 %reduce-scatter.5.cloned.1.call-start = ((), (), s32[]{:S(2)}) async-start(), calls=%async_computation.5 | async-start | bytes 2129920 | tf_op jit(solution)/shard_map/reduce_scatter | solution.py:54
Sparse Core Ops, SparseCore 0:
  10.9 144.1 all-gather.2
  157.3 52.6 all-gather.4
  377.3 24.4 reduce-scatter.2
  410.0 702.5 reduce-scatter.4
where the time goes:
time: 1120 us
  waiting for transfers between devices  914 us (82%)
  blocking collectives  170 us (15%)
  between operations  16.3 us (1%)
  matrix products  14.2 us (1%)
    reduce_scatter x1, waiting for transfers between devices, local(): lax.psum_scatter(hidden_terms, 'vocab', scatter_dimension=1, tiled=True)  688 us
    all_gather x1, waiting for transfers between devices, local(): features = lax.all_gather(hidden, 'vocab', axis=1, tiled=True)  145 us
    psum x1, blocking collectives, local(): scores = lax.psum(partial_value, 'vocab') * inv_root  144 us
    all_gather x1, waiting for transfers between devices, local(): full_head = lax.all_gather(head_weight, 'batch', axis=0, tiled=True)  54.9 us
    reduce_scatter x1, waiting for transfers between devices, local(): lax.psum_scatter(query_terms, 'batch', scatter_dimension=0, tiled=True)  24.6 us
  transfers between devices with their start and end apart: 4, of which 4 were waited for; matrix products, arithmetic and copies ran while one was open for 0% of the time, Pallas kernels for 0%

commit v1 on v0

--- a/solution.py
+++ b/solution.py
@@ -23,7 +23,7 @@
     inv_root = 1.0 / math.sqrt(VOCAB)
     slot_count = pair_query.shape[0]
     is_live = jnp.arange(slot_count, dtype=jnp.int32) < pair_count[0]
-    scores = lax.psum(partial_value, "vocab") * inv_root
+    scores = jnp.sum(lax.all_gather(partial_value, "vocab"), axis=0) * inv_root
     residual = jnp.where(is_live, scores - teacher, 0.0)
     error_total = lax.psum(jnp.sum(residual * residual), "batch")
     pair_grad = 2.0 * residual * inv_root

time: 1120 us -> 1080 us (0.964)
  blocking collectives: 170 us -> 125 us
    psum x1 -> x0, blocking collectives: 144 us -> none  [local(): scores = lax.psum(partial_value, 'vocab') * inv_root]
    all_gather x0 -> x1, blocking collectives: none -> 98.4 us  [local(): scores = jnp.sum(lax.all_gather(partial_value, 'vocab'), axis=0) * inv_root]
where the time goes in v1:
time: 1080 us
  waiting for transfers between devices  919 us (85%)
  blocking collectives  125 us (12%)
  between operations  16.3 us (2%)
  matrix products  14.2 us (1%)
    reduce_scatter x1, waiting for transfers between devices, local(): lax.psum_scatter(hidden_terms, 'vocab', scatter_dimension=1, tiled=True)  687 us
    all_gather x1, waiting for transfers between devices, local(): features = lax.all_gather(hidden, 'vocab', axis=1, tiled=True)  145 us
    all_gather x1, blocking collectives, local(): scores = jnp.sum(lax.all_gather(partial_value, 'vocab'), axis=0) * inv_root  98.4 us
    all_gather x1, waiting for transfers between devices, local(): full_head = lax.all_gather(head_weight, 'batch', axis=0, tiled=True)  54.9 us
    reduce_scatter x1, waiting for transfers between devices, local(): lax.psum_scatter(query_terms, 'batch', scatter_dimension=0, tiled=True)  30.2 us
  transfers between devices with their start and end apart: 4, of which 4 were waited for; matrix products, arithmetic and copies ran while one was open for 0% of the time, Pallas kernels for 0%

profile of v1, /device:TPU:8, one launch (start us, length us, event | category | flops | bytes accessed | tf_op | source)
XLA Modules:
  0.0 1081.4 jit_solution(16888061695690688865)
XLA Ops:
  7.2 0.0 copy-start
  7.2 0.0 all-gather.5.cloned.1.call-start
  7.2 0.7 all-gather.5.cloned.1.call-update
  7.9 0.0 all-gather.7.cloned.1.call-start
  8.0 0.7 all-gather.7.cloned.1.call-update
  8.7 0.0 reduce-scatter.3.cloned.1.call-start
  9.4 0.7 fusion.12
  10.1 0.0 copy-start.2
  10.1 0.0 copy-start.3
  10.1 0.0 copy-start.4
  10.1 145.1 %all-gather.5.cloned.1.call-done = bf16[128,4096]{0,1:T(8,128)(2,1)} async-done(((bf16[128,64]{0,1:T(8,128)(2,1)}), bf16[128,4096]{0,1:T(8,128)(2,1)}) %all-gather.5.cloned.1.call-update) | async-done | bytes 1048592 | tf_op jit(solution)/shard_map/all_gather | solution.py:12
  155.2 54.9 %all-gather.7.cloned.1.call-done = bf16[4096,1024]{1,0:T(8,128)(2,1)} async-done(((bf16[512,1024]{1,0:T(8,128)(2,1)}), bf16[4096,1024]{1,0:T(8,128)(2,1)}) %all-gather.7.cloned.1.call-update) | async-done | bytes 8388624 | tf_op jit(solution)/shard_map/all_gather | solution.py:13
  210.0 5.2 bitcast_reduce_fusion
  215.2 0.0 copy-start.1
  215.2 11.7 %all_gather.17 = bf16[64,1024]{1,0:T(8,128)(2,1)S(1)} all-gather(bf16[8,1024]{1,0:T(8,128)(2,1)S(1)} %get-tuple-element.5), channel_id=1, replica_groups=mesh['vocab'=64,'batch'=8] {'batch'}, dimensions={0}, use_global_device_ids=true | all-gather | bytes 147456 | tf_op jit(solution)/shard_map/all_gather | solution.py:20
  226.9 0.0 copy-done
  226.9 0.3 fusion.16
  227.2 3.4 gather_fusion
  230.7 98.4 %all-gather.1 = f32[64,1,384]{2,1,0:T(1,128)S(1)} all-gather(f32[1,1,384]{2,1,0:T(1,128)S(1)} %reshape.37), channel_id=2, replica_groups=mesh['vocab'=64,'batch'=8] {'vocab'}, dimensions={0}, use_global_device_ids=true | all-gather | bytes 99840 | tf_op jit(solution)/shard_map/all_gather | solution.py:26
  329.1 0.1 reduce_sum.28
  329.1 0.0 copy-done.2
  329.2 0.6 multiply_reduce_fusion
  329.8 0.0 copy-done.3
  329.8 0.0 copy-done.4
  329.8 0.5 fusion.1
  330.3 0.2 fusion.8
  330.5 0.9 convolution_add_fusion
  331.4 0.0 reduce-scatter.3.cloned.1.call-update
  331.5 0.0 reduce-scatter.5.cloned.1.call-start
  331.5 30.2 %reduce-scatter.3.cloned.1.call-done = f32[8,1024]{1,0:T(8,128)} async-done(((f32[64,1024]{1,0:T(8,128)}), f32[8,1024]{1,0:T(8,128)}) %reduce-scatter.3.cloned.1.call-update) | async-done | bytes 32784 | tf_op jit(solution)/shard_map/reduce_scatter | solution.py:45
  361.7 0.9 fusion
  362.6 7.1 fusion.17
  369.7 0.0 copy-done.1
  369.7 0.0 reduce-scatter.5.cloned.1.call-update
  369.8 14.5 %psum.7 = f32[]{:T(128)} all-reduce(f32[]{:T(128)} %get-tuple-element.3), channel_id=1, replica_groups=mesh['vocab'=64,'batch'=8] {'batch'}, use_global_device_ids=true, to_apply=%region_5.6 | all-reduce | flops 1 | bytes 8 | tf_op jit(solution)/shard_map/psum | solution.py:28
  384.9 687.4 %reduce-scatter.5.cloned.1.call-done = f32[128,64]{0,1:T(8,128)} async-done(((f32[128,4096]{0,1:T(8,128)}), f32[128,64]{0,1:T(8,128)}) %reduce-scatter.5.cloned.1.call-update) | async-done | bytes 32784 | tf_op jit(solution)/shard_map/reduce_scatter | solution.py:54
  1072.4 1.4 convert_element_type.25
  (1 shorter events, 0.0 us)
Async XLA Ops:
  7.2 219.8 %copy-start = (bf16[256,1024]{1,0:T(8,128)(2,1)S(1)}, bf16[256,1024]{1,0:T(8,128)(2,1)}, u32[]{:S(2)}) copy-start(bf16[256,1024]{1,0:T(8,128)(2,1)} %param.9) | copy-start | bytes 1572868
  7.2 148.0 %all-gather.5.cloned.1.call-start = ((), (), s32[]{:S(2)}) async-start(), calls=%async_computation.2 | async-start | bytes 1064960 | tf_op jit(solution)/shard_map/all_gather | solution.py:12
  7.9 202.1 %all-gather.7.cloned.1.call-start = ((), (), s32[]{:S(2)}) async-start(), calls=%async_computation.3 | async-start | bytes 9437184 | tf_op jit(solution)/shard_map/all_gather | solution.py:13
  8.7 353.1 %reduce-scatter.3.cloned.1.call-start = ((), (), s32[]{:S(2)}) async-start(), calls=%async_computation.4 | async-start | bytes 294912 | tf_op jit(solution)/shard_map/reduce_scatter | solution.py:45
  10.1 319.1 %copy-start.2 = (f32[384]{0:T(512)S(1)}, f32[384]{0:T(512)}, u32[]{:S(2)}) copy-start(f32[384]{0:T(512)} %param.13) | copy-start | bytes 4612
  10.1 319.7 %copy-start.3 = (s32[384]{0:T(512)S(1)}, s32[384]{0:T(512)}, u32[]{:S(2)}) copy-start(s32[384]{0:T(512)} %param.10) | copy-start | bytes 4612
  10.1 319.7 %copy-start.4 = (s32[384]{0:T(512)S(1)}, s32[384]{0:T(512)}, u32[]{:S(2)}) copy-start(s32[384]{0:T(512)} %param.11) | copy-start | bytes 4612
  215.2 154.5 %copy-start.1 = (bf16[8,1024]{1,0:T(8,128)(2,1)}, bf16[8,1024]{1,0:T(8,128)(2,1)S(1)}, u32[]{:S(2)}) copy-start(bf16[8,1024]{1,0:T(8,128)(2,1)S(1)} %get-tuple-element.5) | copy-start | bytes 49156
  331.5 740.9 %reduce-scatter.5.cloned.1.call-start = ((), (), s32[]{:S(2)}) async-start(), calls=%async_computation.5 | async-start | bytes 2129920 | tf_op jit(solution)/shard_map/reduce_scatter | solution.py:54
Sparse Core Ops, SparseCore 0:
  10.9 144.1 all-gather.4
  157.3 52.6 all-gather.6
  331.6 30.1 reduce-scatter.2
  369.9 702.4 reduce-scatter.4
